TPU v7x, 256 devices: a whole 4x4x8 slice. The times are simulated.
256 devices in a mesh: tiles: 32 (over z, x), sub: 8 (over y, core).
Axes of the slice: x: 4, y: 4, z: 8, core: 2. Of those that a mesh axis runs over, the one named last changes fastest.
Arguments:
- latents: float32 [196608, 512], P(('tiles', 'sub')), may hold values from -130 to 130
- conv_weight: float32 [512, 9, 512], P('tiles'), may hold values from -0.09375 to 0.09375
- conv_bias: float32 [512], replicated, may hold values from -4 to 4
- norm1_gain: float32 [512], replicated, may hold values from 0.5 to 1.5
- norm1_shift: float32 [512], replicated, may hold values from -3 to 3
- norm2_gain: float32 [512], replicated, may hold values from 0.5 to 1.5
- norm2_shift: float32 [512], replicated, may hold values from -3 to 3
- tile_counts: int32 [36], replicated, may hold values from 1 to 64, 768 in all
- widths: int32 [36], replicated, may hold values from 32 to 128, as said below
Outputs:
- activated: float32 [196608, 512], P(('tiles', 'sub'))
Inputs may be any that keep to these rules, and one draw needn't show every extreme that they name: `widths`: each width is 128, 64 or 32; some image has width 128 and some has width 128 / 4. `tile_counts`: they add up to 768; the largest is 64.
All inputs are finite; a program needn't handle non-finite values.
Results may differ from a plain program's by a relative error of at most 0.00014.
Values sent between devices are 32-bit elements; how exact they have to be, the bound alone decides.
A program may use at most 128 MiB of HBM per device.

v0:
```python
import jax
import jax.numpy as jnp
from jax import lax
from jax.sharding import PartitionSpec as P

GROUPS = 32
WMAX = 128
TILE = 256
epsilon = 1e-06
highest = lax.Precision.HIGHEST


def extended(cells, sides, width):
    for axis, dim in sides:
        count = lax.axis_size(axis)
        ends = count - 1
        head = lax.slice_in_dim(cells, 0, width, axis=dim)
        tail = lax.slice_in_dim(cells, cells.shape[dim] - width, cells.shape[dim], axis=dim)
        cells = jnp.concatenate(
            [
                lax.ppermute(tail, axis, [(i, (i + 1) % count) for i in range(ends)]),
                cells,
                lax.ppermute(head, axis, [((i + 1) % count, i) for i in range(ends)]),
            ],
            axis=dim,
        )
    return cells


def pixel_layout(tile_counts, widths, pixels_here):
    device = lax.axis_index("tiles") * lax.axis_size("sub") + lax.axis_index("sub")
    pixel_counts = tile_counts * TILE
    image_ends = jnp.cumsum(pixel_counts)
    image_starts = image_ends - pixel_counts
    position = device * pixels_here + jnp.arange(pixels_here, dtype=jnp.int32)
    member = (position[None, :] >= image_starts[:, None]) & (
        position[None, :] < image_ends[:, None]
    )

    def per_pixel(per_image):
        return jnp.sum(jnp.where(member, per_image[:, None], 0), axis=0)

    pixel_width = per_pixel(widths)
    offset = position - per_pixel(image_starts)
    row_index = offset // pixel_width
    column_index = offset - row_index * pixel_width
    pixel_height = per_pixel(pixel_counts) // pixel_width
    return (
        member.astype(jnp.float32),
        pixel_counts,
        row_index,
        column_index,
        pixel_width,
        pixel_height,
    )


def group_table(per_channel):
    return jnp.sum(per_channel.reshape(per_channel.shape[0], GROUPS, -1), axis=2)


def spread_rows(onehot, per_image):
    return lax.dot_general(
        onehot,
        per_image,
        (((0,), (0,)), ((), ())),
        precision=highest,
        preferred_element_type=jnp.float32,
    )


def normalize(values, norm_gain, norm_shift, onehot, pixel_counts):
    group_size = values.shape[1] // GROUPS
    entries = (pixel_counts * group_size).astype(jnp.float32)[:, None]
    firsts = jnp.dot(onehot, values, precision=highest, preferred_element_type=jnp.float32)
    group_total = lax.psum(group_table(firsts), ("tiles", "sub"))
    group_mean = group_total / entries
    centred = values - spread_rows(onehot, jnp.repeat(group_mean, group_size, axis=1))
    seconds = jnp.dot(
        onehot, centred * centred, precision=highest, preferred_element_type=jnp.float32
    )
    spread = lax.psum(group_table(seconds), ("tiles", "sub")) / entries
    inverse = spread_rows(onehot, jnp.repeat(lax.rsqrt(spread + epsilon), group_size, axis=1))
    return jax.nn.silu(centred * inverse * norm_gain + norm_shift)


def shards(
    latents,
    conv_weight,
    conv_bias,
    norm1_gain,
    norm1_shift,
    norm2_gain,
    norm2_shift,
    tile_counts,
    widths,
):
    pixels_here = latents.shape[0]
    channels = latents.shape[1]
    onehot, pixel_counts, row_index, column_index, pixel_width, pixel_height = pixel_layout(
        tile_counts, widths, pixels_here
    )
    first_act = normalize(latents, norm1_gain, norm1_shift, onehot, pixel_counts)
    padded = extended(first_act.T, ((("tiles", "sub"), 1),), WMAX + 1)
    anchor = jnp.arange(pixels_here, dtype=jnp.int32) + (WMAX + 1)
    sources = []
    validity = []
    for step_y in (-1, 0, 1):
        for step_x in (-1, 0, 1):
            inside = (row_index + step_y >= 0) & (row_index + step_y < pixel_height)
            inside = inside & (column_index + step_x >= 0) & (column_index + step_x < pixel_width)
            sources.append(jnp.where(inside, anchor + step_y * pixel_width + step_x, anchor))
            validity.append(inside.astype(jnp.float32))
    all_sources = jnp.concatenate(sources)
    all_masks = jnp.concatenate(validity)
    tapped = jnp.take(padded, all_sources, axis=1) * all_masks[None, :]
    zero_sum = jnp.zeros((pixels_here, channels), jnp.float32)
    running = zero_sum
    weight_piece = lax.all_gather(conv_weight, "tiles", axis=0, tiled=True)
    row_count = weight_piece.shape[0]
    block_width = min(row_count, 128)
    for block_start in range(0, row_count, block_width):
        block_rows = min(block_width, row_count - block_start)
        taps_block = lax.dynamic_slice_in_dim(tapped, block_start, block_rows, 0)
        taps_block = taps_block.reshape(block_rows, 9, pixels_here)
        weight_block = weight_piece[block_start : block_start + block_rows]
        running = running + jnp.einsum(
            "ktp,kto->po",
            taps_block,
            weight_block,
            precision=highest,
            preferred_element_type=jnp.float32,
        )
    hidden = running
    hidden = hidden + conv_bias
    return normalize(hidden, norm2_gain, norm2_shift, onehot, pixel_counts)


def solution(mesh):
    return jax.shard_map(
        shards,
        mesh=mesh,
        in_specs=(
            P(("tiles", "sub"), None),
            P("tiles", None, None),
            P(),
            P(),
            P(),
            P(),
            P(),
            P(),
            P(),
        ),
        out_specs=P(("tiles", "sub"), None),
        check_vma=False,
    )
```

profile of v0, /device:TPU:1, one launch (start us, length us, event | category | flops | bytes accessed | tf_op | source)
XLA Modules:
  0.0 427.4 jit_solution(8447993397408596706)
XLA Ops:
  6.5 0.0 copy-start.3
  6.5 0.0 all-gather.2.cloned.1.call-start
  6.5 0.7 all-gather.2.cloned.1.call-update
  7.3 0.7 broadcast_multiply_fusion
  7.9 0.1 copy.16
  8.0 0.1 reduce-window.8
  8.1 0.1 reduce
  8.2 0.7 fusion.25
  8.9 2.8 bitcast_reduce_fusion.3
  11.7 83.9 %psum.28 = f32[36,32]{0,1:T(8,128)S(1)} all-reduce(f32[36,32]{0,1:T(8,128)S(1)} %bitcast_reduce_fusion.3), channel_id=1, replica_groups=mesh['tiles'=32,'sub'=8] {'tiles','sub'}, use_global_device_ids=true, to_apply=%region_5.6 | all-reduce | flops 1152 | bytes 9216 | tf_op jit(solution)/shard_map/psum | solution.py:76
  95.6 0.0 copy-done.3
  95.6 0.9 convolution_subtract_fusion.1
  96.6 0.0 copy-start.7
  96.6 0.0 copy-start.8
  96.6 1.4 bitcast_reduce_fusion.2
  98.0 73.4 %psum.29 = f32[36,32]{0,1:T(8,128)S(1)} all-reduce(f32[36,32]{0,1:T(8,128)S(1)} %bitcast_reduce_fusion.2), channel_id=1, replica_groups=mesh['tiles'=32,'sub'=8] {'tiles','sub'}, use_global_device_ids=true, to_apply=%region_7.8 | all-reduce | flops 1152 | bytes 9216 | tf_op jit(solution)/shard_map/psum | solution.py:82
  171.5 0.0 copy-done.7
  171.5 0.0 copy-done.8
  171.5 0.0 copy-start.6
  171.5 1.3 multiply_bitcast_fusion.1
  172.8 0.0 copy-start.4
  172.8 1.1 copy-done.4
  174.0 3.2 collective-permute-start
  177.2 2.4 collective-permute-start.1
  179.6 0.0 copy-done.6
  179.6 0.1 select_reduce_fusion
  179.7 0.1 constant_dynamic-update-slice_fusion
  179.9 0.2 dynamic-update-slice
  180.1 0.2 dynamic-update-slice.1
  180.4 0.2 dynamic-update-slice.2
  180.6 0.1 constant_dynamic-update-slice_fusion.16
  180.8 0.2 dynamic-update-slice.3
  181.0 0.2 dynamic-update-slice.4
  181.3 0.2 dynamic-update-slice.5
  181.5 0.1 constant_dynamic-update-slice_fusion.13
  181.6 0.2 dynamic-update-slice.6
  181.9 0.2 dynamic-update-slice.7
  182.3 0.1 fusion.19
  182.4 0.0 collective-permute-done
  182.4 2.6 collective-permute-done.1
  185.0 4.5 %concatenate.54 = f32[512,1026]{0,1:T(8,128)S(1)} concatenate(f32[512,129]{0,1:T(8,128)S(1)} %collective-permute-done, f32[512,768]{0,1:T(8,128)} %copy-done.4, f32[512,129]{0,1:T(8,128)S(1)} %collective-permute-done.1), dimensions={1} | concatenate | bytes 4202496 | tf_op jit(solution)/shard_map/concatenate | solution.py:19
  189.5 18.6 %gather_fusion = f32[6912,512]{1,0:T(8,128)} fusion(f32[512,1026]{0,1:T(8,128)S(1)} %concatenate.54, s32[7168]{0:T(1024)S(1)} %pad_clamp_fusion), kind=kCustom, calls=%fused_computation | custom fusion | bytes 28339200 | tf_op jit(solution)/shard_map/jit(_take)/gather | solution.py:116
  208.1 11.6 %multiply_bitcast_fusion = f32[512,6912]{0,1:T(8,128)} fusion(f32[6912,512]{1,0:T(8,128)} %gather_fusion, f32[6912]{0:T(1024)S(1)} %concatenate.66, pred[6912]{0:T(1024)(128)(4,1)S(1)} %compare_and_fusion.1), kind=kLoop, calls=%fused_computation.1 | loop fusion | flops 7077888 | bytes 28346112 | tf_op jit(solution)/shard_map/mul | solution.py:116
  219.7 9.4 %fusion.35 = (f32[128,6912]{0,1:T(8,128)}, f32[128,6912]{0,1:T(8,128)}, f32[128,6912]{0,1:T(8,128)}, f32[128,6912]{0,1:T(8,128)S(1)}) fusion(f32[512,6912]{0,1:T(8,128)} %multiply_bitcast_fusion), kind=kLoop, calls=%fused_computation.106 | loop fusion | bytes 28311552 | tf_op jit(solution)/shard_map/dynamic_slice | solution.py:124
  229.1 9.2 %fusion = f32[768,512,1]{1,0,2:T(8,128)S(1)} fusion(f32[128,9,768]{0,2,1:T(8,128)} %bitcast.48, f32[512,9,512]{2,0,1:T(8,128)} %all-gather.2.cloned.1.call-done), kind=kOutput, calls=%fused_computation.2 | convolution fusion | flops 5435817984 | bytes 7471104 | tf_op jit(solution)/shard_map/ktp,kto->po/dot_general | solution.py:127
  238.2 0.0 copy-done
  238.2 8.0 %fusion.2 = f32[768,512,1]{1,0,2:T(8,128)S(1)} fusion(f32[128,9,768]{0,2,1:T(8,128)S(1)} %bitcast.47, f32[512,9,512]{2,0,1:T(8,128)} %all-gather.2.cloned.1.call-done), kind=kOutput, calls=%fused_computation.4 | convolution fusion | flops 5435817984 | bytes 7471104 | tf_op jit(solution)/shard_map/ktp,kto->po/dot_general | solution.py:127
  246.2 0.0 copy-done.2
  246.2 0.0 copy-start.1
  246.3 0.0 copy-start.5
  246.3 6.5 %fusion.4 = f32[768,512,1]{1,0,2:T(8,128)S(1)} fusion(f32[128,9,768]{0,2,1:T(8,128)S(1)} %bitcast.46, f32[512,9,512]{2,0,1:T(8,128)S(1)} %copy-done.2), kind=kOutput, calls=%fused_computation.6 | convolution fusion | flops 5435817984 | bytes 7471104 | tf_op jit(solution)/shard_map/ktp,kto->po/dot_general | solution.py:127
  252.8 0.0 copy-done.1
  252.8 0.0 copy-done.5
  252.8 6.4 %fusion.8 = f32[768,512]{1,0:T(8,128)S(1)} fusion(f32[768,512,1]{1,0,2:T(8,128)S(1)} %fusion, f32[768,512,1]{1,0,2:T(8,128)S(1)} %fusion.2, f32[768,512,1]{1,0,2:T(8,128)S(1)} %fusion.4, f32[128,9,768]{0,2,1:T(8,128)S(1)} %bitcast.49, f32[512,9,512]{2,0,1:T(8,128)S(1)} %copy-done.2, f32[512]{0:T(512)S(1)} %copy-done.5), kind=kOutput, calls=%fused_computation.11 | convolution fusion | flops 5437390848 | bytes 12191744 | tf_op jit(solution)/shard_map/ktp,kto->po/dot_general | solution.py:127
  259.2 1.4 bitcast_reduce_fusion.1
  260.6 82.0 %psum.30 = f32[36,32]{0,1:T(8,128)S(1)} all-reduce(f32[36,32]{0,1:T(8,128)S(1)} %bitcast_reduce_fusion.1), channel_id=1, replica_groups=mesh['tiles'=32,'sub'=8] {'tiles','sub'}, use_global_device_ids=true, to_apply=%region_9.10 | all-reduce | flops 1152 | bytes 9216 | tf_op jit(solution)/shard_map/psum | solution.py:76
  342.6 0.9 convolution_subtract_fusion
  343.6 0.0 copy-start.9
  343.6 0.0 copy-start.10
  343.6 1.4 bitcast_reduce_fusion
  345.0 72.8 %psum.31 = f32[36,32]{0,1:T(8,128)S(1)} all-reduce(f32[36,32]{0,1:T(8,128)S(1)} %bitcast_reduce_fusion), channel_id=1, replica_groups=mesh['tiles'=32,'sub'=8] {'tiles','sub'}, use_global_device_ids=true, to_apply=%region_11.12 | all-reduce | flops 1152 | bytes 9216 | tf_op jit(solution)/shard_map/psum | solution.py:82
  417.9 0.0 copy-done.9
  417.9 0.0 copy-done.10
  417.9 2.4 divide_multiply_fusion
  (37 shorter events, 0.4 us)
Async XLA Ops:
  6.5 89.1 %copy-start.3 = (f32[768,512]{1,0:T(8,128)S(1)}, f32[768,512]{1,0:T(8,128)}, u32[]{:S(2)}) copy-start(f32[768,512]{1,0:T(8,128)} %param.9) | copy-start | bytes 4718596
  6.5 222.5 %all-gather.2.cloned.1.call-start = ((), (), s32[]{:S(2)}) async-start(), calls=%async_computation | async-start | bytes 9732096 | tf_op jit(solution)/shard_map/all_gather | solution.py:119
  96.6 74.9 %copy-start.7 = (f32[512]{0:T(512)S(1)}, f32[512]{0:T(512)}, u32[]{:S(2)}) copy-start(f32[512]{0:T(512)} %param.13) | copy-start | bytes 6148
  96.6 74.9 %copy-start.8 = (f32[512]{0:T(512)S(1)}, f32[512]{0:T(512)}, u32[]{:S(2)}) copy-start(f32[512]{0:T(512)} %param.12) | copy-start | bytes 6148
  171.5 8.1 %copy-start.6 = (s32[36]{0:T(128)S(1)}, s32[36]{0:T(128)}, u32[]{:S(2)}) copy-start(s32[36]{0:T(128)} %param.17) | copy-start | bytes 436
  172.8 1.1 copy-start.4
  174.0 8.5 %collective-permute-start = (f32[512,129]{0,1:T(8,128)S(1)}, f32[512,129]{0,1:T(8,128)S(1)}, u32[]{:S(2)}, u32[]{:S(2)}) collective-permute-start(f32[512,129]{0,1:T(8,128)S(1)} %get-tuple-element.44), channel_id=1, source_target_pairs={{0,1},{1,2},{2,3},{3,4},{4,5},{5,6},{6,7},{7,8},{8,9},{9,10},{10,1... | collective-permute-start | bytes 792584 | tf_op jit(solution)/shard_map/ppermute | solution.py:21
  177.2 7.9 %collective-permute-start.1 = (f32[512,129]{0,1:T(8,128)S(1)}, f32[512,129]{0,1:T(8,128)S(1)}, u32[]{:S(2)}, u32[]{:S(2)}) collective-permute-start(f32[512,129]{0,1:T(8,128)S(1)} %get-tuple-element.43), channel_id=1, source_target_pairs={{1,0},{2,1},{3,2},{4,3},{5,4},{6,5},{7,6},{8,7},{9,8},{10,9},{11,1... | collective-permute-start | bytes 792584 | tf_op jit(solution)/shard_map/ppermute | solution.py:23
  229.1 9.2 %copy-start = (f32[128,6912]{0,1:T(8,128)S(1)}, f32[128,6912]{0,1:T(8,128)}, u32[]{:S(2)}) copy-start(f32[128,6912]{0,1:T(8,128)} %get-tuple-element.41) | copy-start | bytes 10616836
  229.1 17.2 %copy-start.2 = (f32[512,9,512]{2,0,1:T(8,128)S(1)}, f32[512,9,512]{2,0,1:T(8,128)}, u32[]{:S(2)}) copy-start(f32[512,9,512]{2,0,1:T(8,128)} %all-gather.2.cloned.1.call-done) | copy-start | bytes 28311556
  246.2 6.5 %copy-start.1 = (f32[128,6912]{0,1:T(8,128)S(1)}, f32[128,6912]{0,1:T(8,128)}, u32[]{:S(2)}) copy-start(f32[128,6912]{0,1:T(8,128)} %get-tuple-element.39) | copy-start | bytes 10616836
  246.3 6.5 %copy-start.5 = (f32[512]{0:T(512)S(1)}, f32[512]{0:T(512)}, u32[]{:S(2)}) copy-start(f32[512]{0:T(512)} %param.11) | copy-start | bytes 6148
  343.6 74.3 %copy-start.9 = (f32[512]{0:T(512)S(1)}, f32[512]{0:T(512)}, u32[]{:S(2)}) copy-start(f32[512]{0:T(512)} %param.15) | copy-start | bytes 6148
  343.6 74.3 %copy-start.10 = (f32[512]{0:T(512)S(1)}, f32[512]{0:T(512)}, u32[]{:S(2)}) copy-start(f32[512]{0:T(512)} %param.14) | copy-start | bytes 6148
Sparse Core Ops, SparseCore 0:
  9.9 107.2 all-gather.1
where the time goes:
time: 433 us; the launch traced here: 427 us
  blocking collectives  312 us (72%)
  matrix products  42.7 us (10%)
  local copies, waits for them, and re-layouts  35.8 us (8%)
  between operations  14 us (3%)
  other arithmetic  13.9 us (3%)
  starting transfers between devices  5.59 us (1%)
    psum x2, blocking collectives, normalize(): group_total = lax.psum(group_table(firsts), ('tiles', 'sub'))  166 us
    psum x2, blocking collectives, normalize(): spread = lax.psum(group_table(seconds), ('tiles', 'sub')) / entries  146 us
    dot_general x4, matrix products, shards(): jnp.einsum('ktp,kto->po', taps_block, weight_block, precision=highest, pr...  30 us
    gather x1, local copies, waits for them, and re-layouts, shards(): tapped = jnp.take(padded, all_sources, axis=1) * all_masks[None, :]  18.6 us
    mul x1, other arithmetic, shards(): tapped = jnp.take(padded, all_sources, axis=1) * all_masks[None, :]  11.6 us
    dynamic_slice x1, local copies, waits for them, and re-layouts, shards(): taps_block = lax.dynamic_slice_in_dim(tapped, block_start, block_rows, 0)  9.35 us
  transfers between devices with their start and end apart: 3, of which 1 were waited for; matrix products, arithmetic and copies ran while one was open for 13% of the time, Pallas kernels for 0%

commit v1 on v0

--- a/solution.py
+++ b/solution.py
@@ -8,6 +8,11 @@
 TILE = 256
 epsilon = 1e-06
 highest = lax.Precision.HIGHEST
+
+
+def one_after_other(x, one, other):
+    half = lax.psum(x, one)
+    return lax.psum(half, other)
 
 
 def extended(cells, sides, width):
@@ -79,7 +84,7 @@
     seconds = jnp.dot(
         onehot, centred * centred, precision=highest, preferred_element_type=jnp.float32
     )
-    spread = lax.psum(group_table(seconds), ("tiles", "sub")) / entries
+    spread = one_after_other(group_table(seconds), "sub", "tiles") / entries
     inverse = spread_rows(onehot, jnp.repeat(lax.rsqrt(spread + epsilon), group_size, axis=1))
     return jax.nn.silu(centred * inverse * norm_gain + norm_shift)
 

time: 433 us -> 615 us (1.42)
  the two profiles are of different devices: /device:TPU:1 before, /device:TPU:0 now
where the time goes in v1:
time: 615 us; the launch traced here: 606 us
  blocking collectives  496 us (81%)
  matrix products  42.7 us (7%)
  local copies, waits for them, and re-layouts  35.8 us (6%)
  other arithmetic  14.3 us (2%)
  between operations  14.1 us (2%)
    psum x2, blocking collectives, one_after_other(): return lax.psum(half, other)  277 us
    psum x2, blocking collectives, normalize(): group_total = lax.psum(group_table(firsts), ('tiles', 'sub'))  170 us
    psum x2, blocking collectives, one_after_other(): half = lax.psum(x, one)  48.3 us
    dot_general x4, matrix products, shards(): jnp.einsum('ktp,kto->po', taps_block, weight_block, precision=highest, pr...  30 us
    gather x1, local copies, waits for them, and re-layouts, shards(): tapped = jnp.take(padded, all_sources, axis=1) * all_masks[None, :]  18.6 us
  transfers between devices with their start and end apart: 3, of which 0 were waited for; matrix products, arithmetic and copies ran while one was open for 9% of the time, Pallas kernels for 0%

profile of v1, /device:TPU:0, one launch (start us, length us, event | category | flops | bytes accessed | tf_op | source)
XLA Modules:
  0.0 605.9 jit_solution(7930972642001056819)
XLA Ops:
  6.5 0.0 all-gather.2.cloned.1.call-start
  6.5 0.7 all-gather.2.cloned.1.call-update
  7.3 0.7 broadcast_multiply_fusion
  7.9 0.1 copy.16
  8.0 0.1 reduce-window.8
  8.1 0.1 reduce
  8.2 0.7 fusion.25
  8.9 2.9 bitcast_reduce_fusion.3
  11.7 81.9 %psum.42 = f32[36,32]{0,1:T(8,128)S(1)} all-reduce(f32[36,32]{0,1:T(8,128)S(1)} %bitcast_reduce_fusion.3), channel_id=1, replica_groups=mesh['tiles'=32,'sub'=8] {'tiles','sub'}, use_global_device_ids=true, to_apply=%region_5.6 | all-reduce | flops 1152 | bytes 9216 | tf_op jit(solution)/shard_map/psum | solution.py:81
  93.7 0.0 copy-done.3
  93.7 0.9 convolution_subtract_fusion.1
  94.6 0.0 copy-start.7
  94.6 0.0 copy-start.8
  94.6 1.4 bitcast_reduce_fusion.2
  96.1 24.8 %psum.43 = f32[36,32]{0,1:T(8,128)S(1)} all-reduce(f32[36,32]{0,1:T(8,128)S(1)} %bitcast_reduce_fusion.2), channel_id=1, replica_groups=mesh['tiles'=32,'sub'=8] {'sub'}, use_global_device_ids=true, to_apply=%region_7.8 | all-reduce | flops 1152 | bytes 9216 | tf_op jit(solution)/shard_map/psum | solution.py:14
  120.8 138.8 %psum.44 = f32[36,32]{0,1:T(8,128)S(1)} all-reduce(f32[36,32]{0,1:T(8,128)S(1)} %psum.43), channel_id=1, replica_groups=mesh['tiles'=32,'sub'=8] {'tiles'}, use_global_device_ids=true, to_apply=%region_8.9 | all-reduce | flops 1152 | bytes 9216 | tf_op jit(solution)/shard_map/psum | solution.py:15
  259.7 0.0 copy-done.7
  259.7 0.0 copy-done.8
  259.7 0.0 copy-start.6
  259.7 1.3 multiply_bitcast_fusion.1
  261.0 0.0 copy-start.4
  261.0 1.1 copy-done.4
  262.2 1.3 collective-permute-start
  263.5 1.3 collective-permute-start.1
  264.8 0.0 copy-done.6
  264.8 0.1 select_reduce_fusion
  265.0 0.1 constant_dynamic-update-slice_fusion
  265.1 0.2 dynamic-update-slice
  265.4 0.2 dynamic-update-slice.1
  265.6 0.2 dynamic-update-slice.2
  265.9 0.1 constant_dynamic-update-slice_fusion.16
  266.0 0.2 dynamic-update-slice.3
  266.2 0.2 dynamic-update-slice.4
  266.5 0.2 dynamic-update-slice.5
  266.7 0.1 constant_dynamic-update-slice_fusion.13
  266.9 0.2 dynamic-update-slice.6
  267.1 0.2 dynamic-update-slice.7
  267.5 0.1 fusion.19
  267.7 0.0 collective-permute-done
  267.7 0.0 collective-permute-done.1
  267.7 4.5 concatenate.54
  272.2 18.6 %gather_fusion = f32[6912,512]{1,0:T(8,128)} fusion(f32[512,1026]{0,1:T(8,128)S(1)} %concatenate.54, s32[7168]{0:T(1024)S(1)} %pad_clamp_fusion), kind=kCustom, calls=%fused_computation | custom fusion | bytes 28339200 | tf_op jit(solution)/shard_map/jit(_take)/gather | solution.py:121
  290.7 12.1 %multiply_bitcast_fusion = f32[512,6912]{0,1:T(8,128)} fusion(f32[6912,512]{1,0:T(8,128)} %gather_fusion, f32[6912]{0:T(1024)S(1)} %concatenate.66, pred[6912]{0:T(1024)(128)(4,1)S(1)} %compare_and_fusion.1), kind=kLoop, calls=%fused_computation.1 | loop fusion | flops 7077888 | bytes 28346112 | tf_op jit(solution)/shard_map/mul | solution.py:121
  302.8 9.4 %fusion.35 = (f32[128,6912]{0,1:T(8,128)}, f32[128,6912]{0,1:T(8,128)}, f32[128,6912]{0,1:T(8,128)}, f32[128,6912]{0,1:T(8,128)S(1)}) fusion(f32[512,6912]{0,1:T(8,128)} %multiply_bitcast_fusion), kind=kLoop, calls=%fused_computation.106 | loop fusion | bytes 28311552 | tf_op jit(solution)/shard_map/dynamic_slice | solution.py:129
  312.2 9.2 %fusion = f32[768,512,1]{1,0,2:T(8,128)S(1)} fusion(f32[128,9,768]{0,2,1:T(8,128)} %bitcast.48, f32[512,9,512]{2,0,1:T(8,128)} %all-gather.2.cloned.1.call-done), kind=kOutput, calls=%fused_computation.2 | convolution fusion | flops 5435817984 | bytes 7471104 | tf_op jit(solution)/shard_map/ktp,kto->po/dot_general | solution.py:132
  321.4 0.0 copy-done
  321.4 8.0 %fusion.2 = f32[768,512,1]{1,0,2:T(8,128)S(1)} fusion(f32[128,9,768]{0,2,1:T(8,128)S(1)} %bitcast.47, f32[512,9,512]{2,0,1:T(8,128)} %all-gather.2.cloned.1.call-done), kind=kOutput, calls=%fused_computation.4 | convolution fusion | flops 5435817984 | bytes 7471104 | tf_op jit(solution)/shard_map/ktp,kto->po/dot_general | solution.py:132
  329.3 0.0 copy-done.2
  329.4 0.0 copy-start.1
  329.4 0.0 copy-start.5
  329.4 6.5 %fusion.4 = f32[768,512,1]{1,0,2:T(8,128)S(1)} fusion(f32[128,9,768]{0,2,1:T(8,128)S(1)} %bitcast.46, f32[512,9,512]{2,0,1:T(8,128)S(1)} %copy-done.2), kind=kOutput, calls=%fused_computation.6 | convolution fusion | flops 5435817984 | bytes 7471104 | tf_op jit(solution)/shard_map/ktp,kto->po/dot_general | solution.py:132
  335.9 0.0 copy-done.1
  335.9 0.0 copy-done.5
  335.9 6.4 %fusion.8 = f32[768,512]{1,0:T(8,128)S(1)} fusion(f32[768,512,1]{1,0,2:T(8,128)S(1)} %fusion, f32[768,512,1]{1,0,2:T(8,128)S(1)} %fusion.2, f32[768,512,1]{1,0,2:T(8,128)S(1)} %fusion.4, f32[128,9,768]{0,2,1:T(8,128)S(1)} %bitcast.49, f32[512,9,512]{2,0,1:T(8,128)S(1)} %copy-done.2, f32[512]{0:T(512)S(1)} %copy-done.5), kind=kOutput, calls=%fused_computation.11 | convolution fusion | flops 5437390848 | bytes 12191744 | tf_op jit(solution)/shard_map/ktp,kto->po/dot_general | solution.py:132
  342.3 1.4 bitcast_reduce_fusion.1
  343.7 88.0 %psum.45 = f32[36,32]{0,1:T(8,128)S(1)} all-reduce(f32[36,32]{0,1:T(8,128)S(1)} %bitcast_reduce_fusion.1), channel_id=1, replica_groups=mesh['tiles'=32,'sub'=8] {'tiles','sub'}, use_global_device_ids=true, to_apply=%region_10.11 | all-reduce | flops 1152 | bytes 9216 | tf_op jit(solution)/shard_map/psum | solution.py:81
  431.8 0.9 convolution_subtract_fusion
  432.7 0.0 copy-start.9
  432.7 0.0 copy-start.10
  432.7 1.4 bitcast_reduce_fusion
  434.2 23.6 %psum.46 = f32[36,32]{0,1:T(8,128)S(1)} all-reduce(f32[36,32]{0,1:T(8,128)S(1)} %bitcast_reduce_fusion), channel_id=1, replica_groups=mesh['tiles'=32,'sub'=8] {'sub'}, use_global_device_ids=true, to_apply=%region_12.13 | all-reduce | flops 1152 | bytes 9216 | tf_op jit(solution)/shard_map/psum | solution.py:14
  457.7 138.6 %psum.47 = f32[36,32]{0,1:T(8,128)S(1)} all-reduce(f32[36,32]{0,1:T(8,128)S(1)} %psum.46), channel_id=1, replica_groups=mesh['tiles'=32,'sub'=8] {'tiles'}, use_global_device_ids=true, to_apply=%region_13.14 | all-reduce | flops 1152 | bytes 9216 | tf_op jit(solution)/shard_map/psum | solution.py:15
  596.4 0.0 copy-done.9
  596.4 2.4 divide_multiply_fusion
  (39 shorter events, 0.4 us)
Async XLA Ops:
  6.5 87.1 %copy-start.3 = (f32[768,512]{1,0:T(8,128)S(1)}, f32[768,512]{1,0:T(8,128)}, u32[]{:S(2)}) copy-start(f32[768,512]{1,0:T(8,128)} %param.9) | copy-start | bytes 4718596
  6.5 305.6 %all-gather.2.cloned.1.call-start = ((), (), s32[]{:S(2)}) async-start(), calls=%async_computation | async-start | bytes 9732096 | tf_op jit(solution)/shard_map/all_gather | solution.py:124
  94.6 165.1 %copy-start.7 = (f32[512]{0:T(512)S(1)}, f32[512]{0:T(512)}, u32[]{:S(2)}) copy-start(f32[512]{0:T(512)} %param.13) | copy-start | bytes 6148
  94.6 165.1 %copy-start.8 = (f32[512]{0:T(512)S(1)}, f32[512]{0:T(512)}, u32[]{:S(2)}) copy-start(f32[512]{0:T(512)} %param.12) | copy-start | bytes 6148
  259.7 5.1 copy-start.6
  261.0 1.1 copy-start.4
  262.2 5.5 collective-permute-start
  263.5 4.2 collective-permute-start.1
  312.2 9.2 %copy-start = (f32[128,6912]{0,1:T(8,128)S(1)}, f32[128,6912]{0,1:T(8,128)}, u32[]{:S(2)}) copy-start(f32[128,6912]{0,1:T(8,128)} %get-tuple-element.41) | copy-start | bytes 10616836
  312.2 17.2 %copy-start.2 = (f32[512,9,512]{2,0,1:T(8,128)S(1)}, f32[512,9,512]{2,0,1:T(8,128)}, u32[]{:S(2)}) copy-start(f32[512,9,512]{2,0,1:T(8,128)} %all-gather.2.cloned.1.call-done) | copy-start | bytes 28311556
  329.4 6.5 %copy-start.1 = (f32[128,6912]{0,1:T(8,128)S(1)}, f32[128,6912]{0,1:T(8,128)}, u32[]{:S(2)}) copy-start(f32[128,6912]{0,1:T(8,128)} %get-tuple-element.39) | copy-start | bytes 10616836
  329.4 6.5 %copy-start.5 = (f32[512]{0:T(512)S(1)}, f32[512]{0:T(512)}, u32[]{:S(2)}) copy-start(f32[512]{0:T(512)} %param.11) | copy-start | bytes 6148
  432.7 163.7 %copy-start.9 = (f32[512]{0:T(512)S(1)}, f32[512]{0:T(512)}, u32[]{:S(2)}) copy-start(f32[512]{0:T(512)} %param.15) | copy-start | bytes 6148
  432.7 163.7 %copy-start.10 = (f32[512]{0:T(512)S(1)}, f32[512]{0:T(512)}, u32[]{:S(2)}) copy-start(f32[512]{0:T(512)} %param.14) | copy-start | bytes 6148
Sparse Core Ops, SparseCore 0:
  9.9 105.2 all-gather.1
